TPU v7x, 512 devices: a whole 4x8x8 slice. The times are simulated.
512 devices in a mesh: lat: 16 (over x, y_lo, core), lon: 32 (over z, y_hi).
Axes of the slice: x: 4, y: 8 (y_hi: 4, y_lo: 2; y = y_hi * 2 + y_lo), z: 8, core: 2. Of those that a mesh axis runs over, the one named last changes fastest.
Arguments:
- queries: bfloat16 [256, 512, 512], P('lat', 'lon'), may hold values from -12 to 12
- keys: bfloat16 [256, 512, 512], P('lat', 'lon'), may hold values from -12 to 12
- values: bfloat16 [256, 512, 512], P('lat', 'lon'), may hold values from -6 to 6
- out_grad: bfloat16 [256, 512, 512], P('lat', 'lon'), may hold values from -16 to 16
- pos_bias: float32 [8, 13, 13], replicated, may hold values from -0.5 to 0.5
Outputs:
- q_grad: bfloat16 [256, 512, 512], P('lat', 'lon')
- k_grad: bfloat16 [256, 512, 512], P('lat', 'lon')
- v_grad: bfloat16 [256, 512, 512], P('lat', 'lon')
All inputs are finite; a program needn't handle non-finite values.
Results may differ from a plain program's by a relative error of at most 0.006.
Values may be sent and summed in bfloat16 or wider, within the bound.
A program may use at most 64 MiB of HBM per device.

v0:
```python
import functools

import jax
import jax.numpy as jnp
from jax import lax
from jax.experimental import pallas as pl
from jax.experimental.pallas import tpu as pltpu
from jax.sharding import PartitionSpec as P

WINDOW = 13
RADIUS = 6
HEADS = 8
HEAD_DIM = 64
ROWS = 16
COLS = 16
KEY_ROWS = ROWS + 2 * RADIUS
WIDE = 32
BAND = 4
BANDS = ROWS // BAND
DEEP = BAND + 2 * RADIUS
WIDTH = HEADS * HEAD_DIM
OWN = BAND * COLS
NEAR = DEEP * COLS
TOKENS = ROWS * COLS
EDGE = ROWS * RADIUS
RIM = RADIUS * COLS
GROUP = 4
PARTS = HEADS // GROUP
GW = GROUP * HEAD_DIM
QL = GROUP * OWN
EDGE_LANES = GROUP * BAND * RADIUS
STRIP = 384
NEG = -1e30
MESH = pl.DeviceIdType.MESH
F32 = jnp.float32
BF16 = jnp.bfloat16


def iota(shape, dim):
    return lax.broadcasted_iota(jnp.int32, shape, dim)


def sixth(j):
    return lax.shift_right_logical(j * 10923, 16)


def sel(mask):
    return jnp.where(mask, 1.0, 0.0).astype(BF16)


def onehot(rows, cols, target):
    return sel(target == iota((rows, cols), 1))


def dot(a, b):
    return jnp.dot(a, b, preferred_element_type=F32)


def dot_t(a, b):
    return lax.dot_general(a, b, (((1,), (1,)), ((), ())), preferred_element_type=F32)


def t_dot(a, b):
    return lax.dot_general(a, b, (((0,), (0,)), ((), ())), preferred_element_type=F32)


def dot3(a, pick):
    hi = a.astype(BF16)
    rest = a - hi.astype(F32)
    mid = rest.astype(BF16)
    low = (rest - mid.astype(F32)).astype(BF16)
    return dot(hi, pick) + dot(mid, pick) + dot(low, pick)


def edge_token(j, start):
    r = sixth(j)
    return r * COLS + (j - r * RADIUS) + start


def edge_index(token, west, east):
    r = lax.shift_right_logical(token, 4)
    c = lax.bitwise_and(token, 15)
    at = r * RADIUS + c
    in_west = (c >= west) & (c < west + RADIUS)
    in_east = (c >= east) & (c < east + RADIUS)
    return jnp.where(in_west, at - west, jnp.where(in_east, at - east + EDGE, -1))


def pick_lanes(start):
    j = iota((QL, 128), 1)
    return sel((iota((QL, 128), 0) == edge_token(j, start)) & (j < EDGE_LANES))


def put_lanes(start):
    j = iota((128, QL), 0)
    return sel((iota((128, QL), 1) == edge_token(j, start)) & (j < EDGE_LANES))


def combine(a, b, shared):
    m0 = a[0:BANDS]
    m1 = jnp.where(shared, b[0:BANDS], NEG)
    m = jnp.maximum(m0, m1)
    w0 = jnp.exp(m0 - m)
    w1 = jnp.exp(m1 - m)
    total = a[BANDS:2 * BANDS] * w0 + b[BANDS:2 * BANDS] * w1
    weighed = a[2 * BANDS:] * w0 + b[2 * BANDS:] * w1
    return m + jnp.log(total), weighed / total


def kernel(nlat, nlon, q_ref, k_ref, v_ref, g_ref, bias_ref, dq_ref, dk_ref, dv_ref,
           qg, kv, send, land, table, scores, dprobs, srow, final,
           psend, pland, osend, oland, own_dq, halo_dq, dsend, dland, acc, lsend, lland,
           biases, bias, ss, rs, ins):
    lat = lax.axis_index("lat")
    lon = lax.axis_index("lon")
    east = (lat, lax.rem(lon + 1, nlon))
    west = (lat, lax.rem(lon + nlon - 1, nlon))
    north = (lat - 1, lon)
    south = (lat + 1, lon)
    has_north = lat > 0
    has_south = lat < nlat - 1

    loads = [pltpu.make_async_copy(ref, dst, ins.at[i]) for i, (ref, dst) in enumerate((
        (q_ref, qg.at[0, pl.ds(0, ROWS), pl.ds(0, COLS)]),
        (g_ref, qg.at[1, pl.ds(0, ROWS), pl.ds(0, COLS)]),
        (k_ref, kv.at[0, pl.ds(RADIUS, ROWS)]),
        (v_ref, kv.at[1, pl.ds(RADIUS, ROWS)]),
        (bias_ref, bias)))]
    for c in loads:
        c.start()

    bar = pltpu.get_barrier_semaphore()
    pl.semaphore_signal(bar, 1, device_id=east, device_id_type=MESH)
    pl.semaphore_signal(bar, 1, device_id=west, device_id_type=MESH)

    @pl.when(has_north)
    def _():
        pl.semaphore_signal(bar, 1, device_id=north, device_id_type=MESH)

    @pl.when(has_south)
    def _():
        pl.semaphore_signal(bar, 1, device_id=south, device_id_type=MESH)

    def lanes(g):
        return slice(g * GW, (g + 1) * GW)

    def pack_edges(dst, t, tokens, starts):
        for d in range(2):
            pick = onehot(EDGE, TOKENS, edge_token(iota((EDGE, TOKENS), 0), starts[d]))
            got = dot(pick, tokens).astype(BF16)
            for g in range(PARTS):
                dst[g, t, d] = got[:, lanes(g)]

    for t in range(2):
        loads[t].wait()
        tokens = qg[t, :, 0:COLS, :].reshape(TOKENS, WIDTH)
        pack_edges(send, t, tokens, (COLS - RADIUS, 0))
    for c in loads[2:]:
        c.wait()
    peers = 2 + has_north.astype(jnp.int32) + has_south.astype(jnp.int32)
    pl.semaphore_wait(bar, peers)

    along = (east, west)
    across = (south, north)

    def remote(g, i, src, dst, to):
        return pltpu.make_async_remote_copy(
            src, dst, ss.at[g, i], rs.at[g, i], device_id=to, device_id_type=MESH)

    def lon_copy(g, t, d):
        return remote(g, 2 * t + d, send.at[g, t, d], land.at[g, t, d], along[d])

    def kv_mid(g):
        span = pl.ds(g * GW, GW)
        return lambda d: [remote(
            g, 4 + 2 * t + d,
            kv.at[t, pl.ds(ROWS if d == 0 else RADIUS, RADIUS), pl.ds(0, COLS), span],
            kv.at[t, pl.ds(0 if d == 0 else ROWS + RADIUS, RADIUS), pl.ds(0, COLS), span],
            across[d]) for t in range(2)]

    def own_copy(g, d):
        return remote(g, 8 + d, osend.at[g, d], oland.at[g, d], along[d])

    def part_copy(g, d):
        return remote(g, 10 + d, psend.at[g, d], pland.at[g, d], along[d])

    def dq_copy(g, d):
        return remote(g, 12 + d, dsend.at[g, 0, d], dland.at[g, d], along[d])

    def lat_back(g):
        return lambda d: [remote(g, 14 + d, lsend.at[g, d], lland.at[g, d], across[d])]

    out_ok = (has_south, has_north)
    in_ok = (has_north, has_south)

    def lat_do(make, ok, what):
        for d in range(2):
            @pl.when(ok[d])
            def _(d=d):
                for c in make(d):
                    what(c)

    def start_lat(make):
        lat_do(make, out_ok, lambda c: c.start())

    def recv_lat(make):
        lat_do(make, in_ok, lambda c: c.wait_recv())

    def sent_lat(make):
        lat_do(make, out_ok, lambda c: c.wait_send())

    def start_lon(g):
        for t in range(2):
            for d in range(2):
                lon_copy(g, t, d).start()

    start_lat(kv_mid(0))
    start_lat(kv_mid(1))
    start_lon(0)
    start_lon(1)

    @pl.when(jnp.logical_not(has_north))
    def _():
        kv[:, 0:RADIUS] = jnp.zeros((2, RADIUS, COLS, WIDTH), BF16)

    @pl.when(jnp.logical_not(has_south))
    def _():
        kv[:, RADIUS + ROWS:KEY_ROWS] = jnp.zeros((2, RADIUS, COLS, WIDTH), BF16)

    acc[...] = jnp.zeros((2, KEY_ROWS * COLS, WIDTH), F32)

    biases[...] = jnp.zeros((128, 128), F32)
    for a in range(WINDOW):
        biases[a * HEADS:(a + 1) * HEADS, 0:WINDOW] = bias[a]
    turned = jnp.transpose(biases[...])[0:16, :]
    row = iota((128, STRIP), 0)
    step = 15 - lax.shift_right_logical(iota((128, STRIP), 1), 4)
    w = lax.shift_right_logical(iota((COLS, STRIP), 1), 4)
    cc = lax.bitwise_and(iota((COLS, STRIP), 1), 15)
    in_window = (w >= 3) & (w < 3 + WINDOW)
    key_col = iota((COLS, STRIP), 0) + RADIUS
    halo_col = jnp.where(cc < RADIUS, cc - RADIUS, cc + COLS - RADIUS)
    offsets = (jnp.where(in_window, key_col - cc, -1),
               jnp.where(in_window & (cc < 2 * RADIUS), key_col - halo_col, -1))
    for h in range(HEADS):
        spread = dot3(turned, sel(row == step * HEADS + h))
        for half in range(2):
            strip = jnp.full((COLS, STRIP), NEG, F32)
            for b in range(WINDOW):
                strip = jnp.where(offsets[half] == b, spread[b:b + 1, :], strip)
            for r in range(DEEP):
                shift = (DEEP - 1 - r) * COLS
                moved = pltpu.roll(strip, STRIP - shift, 1) if shift else strip
                table[half, r * COLS:(r + 1) * COLS, h * OWN:(h + 1) * OWN] = moved[:, :OWN]

    head_of = lax.shift_right_logical(iota((1, GW), 1), 6)
    keep = [jnp.where(head_of == hh, 1.0, 0.0) for hh in range(GROUP)]
    keep_low = [m.astype(BF16) for m in keep]
    scale = HEAD_DIM ** -0.5

    def stack(x):
        return jnp.concatenate([x * m for m in keep_low], axis=0)

    def unstack(y):
        total = y[0:OWN] * keep[0]
        for hh in range(1, GROUP):
            total = total + y[hh * OWN:(hh + 1) * OWN] * keep[hh]
        return total

    def operands(half, g, lo):
        cols = pl.ds(half * COLS, COLS)
        qt = qg[0, pl.ds(lo, BAND), cols, lanes(g)].reshape(OWN, GW) * scale
        gt = qg[1, pl.ds(lo, BAND), cols, lanes(g)].reshape(OWN, GW)
        kt = kv[0, pl.ds(lo, DEEP), :, lanes(g)].reshape(NEAR, GW)
        return stack(qt.astype(BF16)), stack(gt), kt

    hide_north = jnp.where(has_north, 0.0, NEG)
    hide_south = jnp.where(has_south, 0.0, NEG)

    def score(half, g):
        def body(band):
            lo = band * BAND
            qs, gs, kt = operands(half, g, lo)
            vt = kv[1, pl.ds(lo, DEEP), :, lanes(g)].reshape(NEAR, GW)
            s = dot_t(kt, qs) + table[half, :, g * QL:(g + 1) * QL]
            above = max(RADIUS - lo, 0) * COLS
            below = min(RADIUS + ROWS - lo, DEEP) * COLS
            if above:
                s = jnp.concatenate([s[:above] + hide_north, s[above:]], axis=0)
            if below < NEAR:
                s = jnp.concatenate([s[:below], s[below:] + hide_south], axis=0)
            dp = dot_t(vt, gs)
            scores[half, g * BANDS + band] = s
            dprobs[half, g * BANDS + band] = dp
            m = jnp.max(s, axis=0, keepdims=True)
            e = jnp.exp(s - m)
            srow[half, g, pl.ds(band, 1), :] = m
            srow[half, g, pl.ds(BANDS + band, 1), :] = jnp.sum(e, axis=0, keepdims=True)
            srow[half, g, pl.ds(2 * BANDS + band, 1), :] = jnp.sum(e * dp, axis=0, keepdims=True)

        for band in range(BANDS):
            body(band)
        return srow[half, g, 0:3 * BANDS, :]

    def grad(half, g):
        def body(band):
            lo = band * BAND
            qs, gs, kt = operands(half, g, lo)
            p = jnp.exp(scores[half, g * BANDS + band] - final[half, g, pl.ds(band, 1), :])
            gap = dprobs[half, g * BANDS + band] - final[half, g, pl.ds(BANDS + band, 1), :]
            ds = (p * gap).astype(BF16)
            keys = pl.ds(lo * COLS, NEAR)
            acc[0, keys, lanes(g)] += dot(ds, qs)
            acc[1, keys, lanes(g)] += dot(p.astype(BF16), gs)
            dq = unstack(t_dot(ds, kt)) * scale
            at = pl.ds(band * OWN, OWN)
            if half:
                halo_dq[at, lanes(g)] = dq.astype(BF16)
            else:
                own_dq[at, lanes(g)] = dq

        for band in range(BANDS):
            body(band)

    column = lax.bitwise_and(iota((BANDS, QL), 1), 15)
    spread_lon = onehot(TOKENS, 2 * EDGE, edge_index(iota((TOKENS, 2 * EDGE), 0), 0, RADIUS))
    mine = {}
    parts = {}

    def own_scores(g):
        recv_lat(kv_mid(g))
        mine[g] = score(0, g)
        for d in range(2):
            osend[g, d] = dot3(mine[g], pick_lanes(COLS - RADIUS if d == 0 else 0))
        for d in range(2):
            own_copy(g, d).start()

    def halo_scores(g):
        for t in range(2):
            for d in range(2):
                lon_copy(g, t, d).wait_recv()
            got = dot(spread_lon, land[g, t].reshape(2 * EDGE, GW)).astype(BF16)
            qg[t, :, COLS:WIDE, lanes(g)] = got.reshape(ROWS, 16, GW)
        parts[g] = score(1, g)
        for d in range(2):
            psend[g, d] = dot3(parts[g], pick_lanes(RADIUS if d == 0 else 0))
        for d in range(2):
            part_copy(g, d).start()

    def halo_grads(g):
        theirs = jnp.zeros((3 * BANDS, QL), F32)
        for d in range(2):
            own_copy(g, d).wait_recv()
            theirs = theirs + dot3(oland[g, d], put_lanes(d * RADIUS))
        held = column < 2 * RADIUS
        lse, delta = combine(parts[g], theirs, held)
        final[1, g, 0:BANDS, :] = jnp.where(held, lse, 0.0)
        final[1, g, BANDS:2 * BANDS, :] = jnp.where(held, delta, 0.0)
        grad(1, g)
        for d in range(2):
            start = RADIUS if d == 0 else 0
            pick = onehot(EDGE, TOKENS, edge_token(iota((EDGE, TOKENS), 0), start))
            dsend[g, 0, d] = dot(pick, halo_dq[:, lanes(g)]).astype(BF16)
        for d in range(2):
            dq_copy(g, d).start()

    def own_grads(g):
        theirs = jnp.zeros((3 * BANDS, QL), F32)
        for d in range(2):
            part_copy(g, d).wait_recv()
            theirs = theirs + dot3(pland[g, d], put_lanes(0 if d == 0 else COLS - RADIUS))
        lse, delta = combine(mine[g], theirs, (column < RADIUS) | (column >= COLS - RADIUS))
        final[0, g, 0:BANDS, :] = lse
        final[0, g, BANDS:2 * BANDS, :] = delta
        grad(0, g)
        for t in range(2):
            lsend[g, 0, t] = acc[t, KEY_ROWS * COLS - RIM:, lanes(g)].astype(BF16)
            lsend[g, 1, t] = acc[t, 0:RIM, lanes(g)].astype(BF16)
        start_lat(lat_back(g))

    own_scores(0)
    own_scores(1)
    halo_scores(0)
    halo_scores(1)
    halo_grads(0)
    halo_grads(1)
    own_grads(0)
    own_grads(1)

    spread_dq = onehot(TOKENS, 2 * EDGE,
                       edge_index(iota((TOKENS, 2 * EDGE), 0), 0, COLS - RADIUS))
    for g in range(PARTS):
        for d in range(2):
            dq_copy(g, d).wait_recv()
        dq = own_dq[:, lanes(g)] + dot(spread_dq, dland[g].reshape(2 * EDGE, GW))
        dq_ref[:, :, lanes(g)] = dq.astype(BF16).reshape(ROWS, COLS, GW)
    for g in range(PARTS):
        recv_lat(lat_back(g))
        for t, out in enumerate((dk_ref, dv_ref)):
            first, last = RIM, RIM + TOKENS
            top = acc[t, first:first + RIM, lanes(g)]
            top = top + jnp.where(has_north, lland[g, 0, t].astype(F32), 0.0)
            bottom = acc[t, last - RIM:last, lanes(g)]
            bottom = bottom + jnp.where(has_south, lland[g, 1, t].astype(F32), 0.0)
            middle = acc[t, first + RIM:last - RIM, lanes(g)]
            out[0:RADIUS, :, lanes(g)] = top.astype(BF16).reshape(RADIUS, COLS, GW)
            out[RADIUS:ROWS - RADIUS, :, lanes(g)] = middle.astype(BF16).reshape(
                ROWS - 2 * RADIUS, COLS, GW)
            out[ROWS - RADIUS:ROWS, :, lanes(g)] = bottom.astype(BF16).reshape(RADIUS, COLS, GW)

    for g in range(PARTS):
        for d in range(2):
            for t in range(2):
                lon_copy(g, t, d).wait_send()
            own_copy(g, d).wait_send()
            part_copy(g, d).wait_send()
            dq_copy(g, d).wait_send()
        sent_lat(kv_mid(g))
        sent_lat(lat_back(g))


def hand_on(*refs):
    for i in range(3):
        refs[3 + i][...] = refs[i][...]


def on_device(nlat, nlon, queries, keys, values, out_grad, pos_bias):
    block = jax.ShapeDtypeStruct((ROWS, COLS, WIDTH), BF16)
    vmem = pl.BlockSpec(memory_space=pltpu.VMEM)
    dma = pltpu.SemaphoreType.DMA
    args = (queries, keys, values, out_grad, jnp.transpose(pos_bias, (1, 0, 2)))
    args = [pltpu.with_memory_space_constraint(x, pltpu.HBM) for x in args]
    grads = pl.pallas_call(
        functools.partial(kernel, nlat, nlon),
        out_shape=(block, block, block),
        in_specs=[pl.BlockSpec(memory_space=pltpu.HBM)] * 5,
        out_specs=(vmem,) * 3,
        scratch_shapes=[
            pltpu.VMEM((2, ROWS, WIDE, WIDTH), BF16),
            pltpu.VMEM((2, KEY_ROWS, COLS, WIDTH), BF16),
            pltpu.VMEM((PARTS, 2, 2, EDGE, GW), BF16),
            pltpu.VMEM((PARTS, 2, 2, EDGE, GW), BF16),
            pltpu.VMEM((2, NEAR, HEADS * OWN), F32),
            pltpu.VMEM((2, PARTS * BANDS, NEAR, QL), F32),
            pltpu.VMEM((2, PARTS * BANDS, NEAR, QL), F32),
            pltpu.VMEM((2, PARTS, 16, QL), F32),
            pltpu.VMEM((2, PARTS, 8, QL), F32),
            pltpu.VMEM((PARTS, 2, 3 * BANDS, 128), F32),
            pltpu.VMEM((PARTS, 2, 3 * BANDS, 128), F32),
            pltpu.VMEM((PARTS, 2, 3 * BANDS, 128), F32),
            pltpu.VMEM((PARTS, 2, 3 * BANDS, 128), F32),
            pltpu.VMEM((TOKENS, WIDTH), F32),
            pltpu.VMEM((TOKENS, WIDTH), BF16),
            pltpu.VMEM((PARTS, 1, 2, EDGE, GW), BF16),
            pltpu.VMEM((PARTS, 2, EDGE, GW), BF16),
            pltpu.VMEM((2, KEY_ROWS * COLS, WIDTH), F32),
            pltpu.VMEM((PARTS, 2, 2, RIM, GW), BF16),
            pltpu.VMEM((PARTS, 2, 2, RIM, GW), BF16),
            pltpu.VMEM((128, 128), F32),
            pltpu.VMEM((WINDOW, HEADS, WINDOW), F32),
            dma((PARTS, 16)),
            dma((PARTS, 16)),
            dma((5,)),
        ],
        name="neighbourhood",
        compiler_params=pltpu.CompilerParams(
            collective_id=0, has_side_effects=True, vmem_limit_bytes=40 * 1024 * 1024),
    )(*args)
    return pl.pallas_call(
        hand_on,
        out_shape=(block, block, block),
        in_specs=[vmem] * 3,
        out_specs=(vmem,) * 3,
        name="hand_on",
        compiler_params=pltpu.CompilerParams(vmem_limit_bytes=8 * 1024 * 1024),
    )(*grads)


def solution(mesh):
    spec = P("lat", "lon", None)
    return jax.shard_map(
        functools.partial(on_device, mesh.shape["lat"], mesh.shape["lon"]),
        mesh=mesh,
        in_specs=(spec, spec, spec, spec, P()),
        out_specs=(spec, spec, spec),
        check_vma=False,
    )
```

profile of v0, /device:TPU:13, one launch (start us, length us, event | category | flops | bytes accessed | tf_op | source)
XLA Modules:
  0.0 41.6 jit_solution(11506164639013010652)
XLA Ops:
  0.6 40.0 %neighbourhood.1 = (bf16[16,16,512]{2,1,0:T(8,128)(2,1)S(1)}, bf16[16,16,512]{2,1,0:T(8,128)(2,1)S(1)}, bf16[16,16,512]{2,1,0:T(8,128)(2,1)S(1)}) custom-call(bf16[16,16,512]{2,1,0:T(8,128)(2,1)} %q_ref.1, bf16[16,16,512]{2,1,0:T(8,128)(2,1)} %k_ref.1, bf16[16,16,512]{2,1,0:T(8,128)(2,1)} %v_ref.1, bf16[16,16,512]{2,1,0:T(8,128)(2,1)} %g_ref.1, ...), custom_call_target="tpu_custom_call" | custom-call | tf_op jit(solution)/shard_map/neighbourhood/pallas_call | solution.py:433
  40.7 0.9 %hand_on.1 = (bf16[16,16,512]{2,1,0:T(8,128)(2,1)}, bf16[16,16,512]{2,1,0:T(8,128)(2,1)}, bf16[16,16,512]{2,1,0:T(8,128)(2,1)}) custom-call(bf16[16,16,512]{2,1,0:T(8,128)(2,1)S(1)} %get-tuple-element.6.refs_0_, bf16[16,16,512]{2,1,0:T(8,128)(2,1)S(1)} %get-tuple-element.7.refs_1_, bf16[16,16,512]{2,1,0:T(8,128)(2,1)S(1)} %get-tuple-element.8.refs_2_), custom_call_target="tpu_custom_call" | custom-call | tf_op jit(solution)/shard_map/hand_on/pallas_call | solution.py:469
where the time goes:
time: 41.7 us; the launch traced here: 41.6 us
  Pallas kernels  41 us (98%)
  between operations  0.64 us (2%)
    pallas_call x1, Pallas kernels, on_device(): pl.pallas_call(functools.partial(kernel, nlat, nlon), out_shape=(block, b...  40 us
    pallas_call x1, Pallas kernels, on_device(): pl.pallas_call(hand_on, out_shape=(block, block, block), in_specs=[vmem]...  0.93 us

commit v1 on v0

--- a/solution.py
+++ b/solution.py
@@ -28,7 +28,8 @@
 PARTS = HEADS // GROUP
 GW = GROUP * HEAD_DIM
 QL = GROUP * OWN
-EDGE_LANES = GROUP * BAND * RADIUS
+SIDE = 8
+SL = GROUP * BAND * SIDE
 STRIP = 384
 NEG = -1e30
 MESH = pl.DeviceIdType.MESH
@@ -86,14 +87,17 @@
     return jnp.where(in_west, at - west, jnp.where(in_east, at - east + EDGE, -1))
 
 
+def side_lane(j, start):
+    c = lax.bitwise_and(j, SIDE - 1)
+    return jnp.where(c < RADIUS, lax.shift_right_logical(j, 3) * COLS + c + start, -1)
+
+
 def pick_lanes(start):
-    j = iota((QL, 128), 1)
-    return sel((iota((QL, 128), 0) == edge_token(j, start)) & (j < EDGE_LANES))
+    return sel(iota((QL, SL), 0) == side_lane(iota((QL, SL), 1), start))
 
 
 def put_lanes(start):
-    j = iota((128, QL), 0)
-    return sel((iota((128, QL), 1) == edge_token(j, start)) & (j < EDGE_LANES))
+    return sel(iota((SL, QL), 1) == side_lane(iota((SL, QL), 0), start))
 
 
 def combine(a, b, shared):
@@ -108,7 +112,7 @@
 
 
 def kernel(nlat, nlon, q_ref, k_ref, v_ref, g_ref, bias_ref, dq_ref, dk_ref, dv_ref,
-           qg, kv, send, land, table, scores, dprobs, srow, final,
+           qg, kv, send, land, table, rim_table, scores, rim_scores, rim_dprobs, dprobs, srow, final,
            psend, pland, osend, oland, own_dq, halo_dq, dsend, dland, acc, lsend, lland,
            biases, bias, ss, rs, ins):
     lat = lax.axis_index("lat")
@@ -227,7 +231,7 @@
     def _():
         kv[:, RADIUS + ROWS:KEY_ROWS] = jnp.zeros((2, RADIUS, COLS, WIDTH), BF16)
 
-    acc[...] = jnp.zeros((2, KEY_ROWS * COLS, WIDTH), F32)
+    acc[...] = jnp.zeros((2, KEY_ROWS, COLS, WIDTH), F32)
 
     biases[...] = jnp.zeros((128, 128), F32)
     for a in range(WINDOW):
@@ -238,20 +242,34 @@
     w = lax.shift_right_logical(iota((COLS, STRIP), 1), 4)
     cc = lax.bitwise_and(iota((COLS, STRIP), 1), 15)
     in_window = (w >= 3) & (w < 3 + WINDOW)
-    key_col = iota((COLS, STRIP), 0) + RADIUS
-    halo_col = jnp.where(cc < RADIUS, cc - RADIUS, cc + COLS - RADIUS)
-    offsets = (jnp.where(in_window, key_col - cc, -1),
-               jnp.where(in_window & (cc < 2 * RADIUS), key_col - halo_col, -1))
+    offset = jnp.where(in_window, iota((COLS, STRIP), 0) + RADIUS - cc, -1)
+    rim_step = 15 - lax.shift_right_logical(iota((128, 256), 1), 3)
+    rim_row = iota((128, 256), 0)
+    w = lax.shift_right_logical(iota((2 * SIDE, 256), 1), 3)
+    cc = lax.bitwise_and(iota((2 * SIDE, 256), 1), SIDE - 1)
+    key_col = iota((2 * SIDE, 256), 0)
+    far = jnp.where(key_col < SIDE, cc - RADIUS, cc + COLS)
+    rim_known = (w >= 3) & (w < 3 + WINDOW) & (cc < RADIUS)
+    rim_offset = jnp.where(rim_known, key_col - far + RADIUS, -1)
     for h in range(HEADS):
         spread = dot3(turned, sel(row == step * HEADS + h))
-        for half in range(2):
-            strip = jnp.full((COLS, STRIP), NEG, F32)
-            for b in range(WINDOW):
-                strip = jnp.where(offsets[half] == b, spread[b:b + 1, :], strip)
-            for r in range(DEEP):
-                shift = (DEEP - 1 - r) * COLS
-                moved = pltpu.roll(strip, STRIP - shift, 1) if shift else strip
-                table[half, r * COLS:(r + 1) * COLS, h * OWN:(h + 1) * OWN] = moved[:, :OWN]
+        strip = jnp.full((COLS, STRIP), NEG, F32)
+        for b in range(WINDOW):
+            strip = jnp.where(offset == b, spread[b:b + 1, :], strip)
+        for r in range(DEEP):
+            shift = (DEEP - 1 - r) * COLS
+            moved = pltpu.roll(strip, STRIP - shift, 1) if shift else strip
+            table[r * COLS:(r + 1) * COLS, h * OWN:(h + 1) * OWN] = moved[:, :OWN]
+        spread = dot3(turned, sel(rim_row == rim_step * HEADS + h))
+        strip = jnp.full((2 * SIDE, 256), NEG, F32)
+        for b in range(WINDOW):
+            strip = jnp.where(rim_offset == b, spread[b:b + 1, :], strip)
+        for r in range(DEEP):
+            shift = (DEEP - 1 - r) * SIDE
+            moved = pltpu.roll(strip, 256 - shift, 1) if shift else strip
+            for side in range(2):
+                rim_table[side, r * SIDE:(r + 1) * SIDE, h * 32:(h + 1) * 32] = (
+                    moved[side * SIDE:(side + 1) * SIDE, :32])
 
     head_of = lax.shift_right_logical(iota((1, GW), 1), 6)
     keep = [jnp.where(head_of == hh, 1.0, 0.0) for hh in range(GROUP)]
@@ -262,68 +280,91 @@
         return jnp.concatenate([x * m for m in keep_low], axis=0)
 
     def unstack(y):
-        total = y[0:OWN] * keep[0]
+        n = y.shape[0] // GROUP
+        total = y[0:n] * keep[0]
         for hh in range(1, GROUP):
-            total = total + y[hh * OWN:(hh + 1) * OWN] * keep[hh]
+            total = total + y[hh * n:(hh + 1) * n] * keep[hh]
         return total
+
+    def side_of(x, side):
+        rows = x.shape[0] * SIDE
+        return x.astype(F32)[:, side * SIDE:(side + 1) * SIDE, :].reshape(rows, GW)
 
     def operands(half, g, lo):
         cols = pl.ds(half * COLS, COLS)
-        qt = qg[0, pl.ds(lo, BAND), cols, lanes(g)].reshape(OWN, GW) * scale
-        gt = qg[1, pl.ds(lo, BAND), cols, lanes(g)].reshape(OWN, GW)
-        kt = kv[0, pl.ds(lo, DEEP), :, lanes(g)].reshape(NEAR, GW)
-        return stack(qt.astype(BF16)), stack(gt), kt
+        tiles = (qg[0, lo:lo + BAND, cols, lanes(g)], qg[1, lo:lo + BAND, cols, lanes(g)],
+                 kv[0, lo:lo + DEEP, :, lanes(g)], kv[1, lo:lo + DEEP, :, lanes(g)])
+        if half:
+            sets = [[side_of(x, side) for x in tiles] for side in range(2)]
+        else:
+            sets = [[x.reshape(x.shape[0] * COLS, GW) for x in tiles]]
+        return [(stack((q * scale).astype(BF16)), stack(g.astype(BF16)), k.astype(BF16),
+                 v.astype(BF16)) for q, g, k, v in sets]
 
     hide_north = jnp.where(has_north, 0.0, NEG)
     hide_south = jnp.where(has_south, 0.0, NEG)
 
     def score(half, g):
-        def body(band):
+        for band in range(BANDS):
             lo = band * BAND
-            qs, gs, kt = operands(half, g, lo)
-            vt = kv[1, pl.ds(lo, DEEP), :, lanes(g)].reshape(NEAR, GW)
-            s = dot_t(kt, qs) + table[half, :, g * QL:(g + 1) * QL]
-            above = max(RADIUS - lo, 0) * COLS
-            below = min(RADIUS + ROWS - lo, DEEP) * COLS
-            if above:
-                s = jnp.concatenate([s[:above] + hide_north, s[above:]], axis=0)
-            if below < NEAR:
-                s = jnp.concatenate([s[:below], s[below:] + hide_south], axis=0)
-            dp = dot_t(vt, gs)
-            scores[half, g * BANDS + band] = s
-            dprobs[half, g * BANDS + band] = dp
-            m = jnp.max(s, axis=0, keepdims=True)
-            e = jnp.exp(s - m)
-            srow[half, g, pl.ds(band, 1), :] = m
-            srow[half, g, pl.ds(BANDS + band, 1), :] = jnp.sum(e, axis=0, keepdims=True)
-            srow[half, g, pl.ds(2 * BANDS + band, 1), :] = jnp.sum(e * dp, axis=0, keepdims=True)
-
+            for side, (qs, gs, kt, vt) in enumerate(operands(half, g, lo)):
+                if half:
+                    bias_of = rim_table[side, :, g * SL:(g + 1) * SL]
+                else:
+                    bias_of = table[:, g * QL:(g + 1) * QL]
+                s = dot_t(kt, qs) + bias_of
+                width = kt.shape[0] // DEEP
+                above = max(RADIUS - lo, 0) * width
+                below = min(RADIUS + ROWS - lo, DEEP) * width
+                if above:
+                    s = jnp.concatenate([s[:above] + hide_north, s[above:]], axis=0)
+                if below < DEEP * width:
+                    s = jnp.concatenate([s[:below], s[below:] + hide_south], axis=0)
+                dp = dot_t(vt, gs)
+                if half:
+                    rim_scores[g * BANDS + band, side] = s
+                    rim_dprobs[g * BANDS + band, side] = dp
+                else:
+                    scores[g * BANDS + band] = s
+                    dprobs[g * BANDS + band] = dp
+                m = jnp.max(s, axis=0, keepdims=True)
+                e = jnp.exp(s - m)
+                at = slice(side * SL, side * SL + s.shape[1])
+                srow[half, g, band:band + 1, at] = m
+                srow[half, g, BANDS + band:BANDS + band + 1, at] = jnp.sum(
+                    e, axis=0, keepdims=True)
+                srow[half, g, 2 * BANDS + band:2 * BANDS + band + 1, at] = jnp.sum(
+                    e * dp, axis=0, keepdims=True)
+        return srow[half, g, 0:3 * BANDS, :]
+
+    def grad(half, g):
         for band in range(BANDS):
-            body(band)
-        return srow[half, g, 0:3 * BANDS, :]
-
-    def grad(half, g):
-        def body(band):
             lo = band * BAND
-            qs, gs, kt = operands(half, g, lo)
-            p = jnp.exp(scores[half, g * BANDS + band] - final[half, g, pl.ds(band, 1), :])
-            gap = dprobs[half, g * BANDS + band] - final[half, g, pl.ds(BANDS + band, 1), :]
-            ds = (p * gap).astype(BF16)
-            keys = pl.ds(lo * COLS, NEAR)
-            acc[0, keys, lanes(g)] += dot(ds, qs)
-            acc[1, keys, lanes(g)] += dot(p.astype(BF16), gs)
-            dq = unstack(t_dot(ds, kt)) * scale
-            at = pl.ds(band * OWN, OWN)
+            dqs = []
+            for side, (qs, gs, kt, _) in enumerate(operands(half, g, lo)):
+                at = slice(side * SL, side * SL + qs.shape[0])
+                lse = final[half, g, band:band + 1, at]
+                delta = final[half, g, BANDS + band:BANDS + band + 1, at]
+                if half:
+                    s, dp = rim_scores[g * BANDS + band, side], rim_dprobs[g * BANDS + band, side]
+                else:
+                    s, dp = scores[g * BANDS + band], dprobs[g * BANDS + band]
+                p = jnp.exp(s - lse)
+                ds = (p * (dp - delta)).astype(BF16)
+                width = kt.shape[0] // DEEP
+                cols = slice(side * SIDE, side * SIDE + width)
+                dk, dv = dot(ds, qs), dot(p.astype(BF16), gs)
+                acc[0, lo:lo + DEEP, cols, lanes(g)] += dk.reshape(DEEP, width, GW)
+                acc[1, lo:lo + DEEP, cols, lanes(g)] += dv.reshape(DEEP, width, GW)
+                dqs.append((unstack(t_dot(ds, kt)) * scale).reshape(BAND, width, GW))
             if half:
-                halo_dq[at, lanes(g)] = dq.astype(BF16)
+                both = jnp.concatenate(dqs, axis=1)
+                halo_dq[band * OWN:(band + 1) * OWN, lanes(g)] = both.reshape(OWN, GW).astype(BF16)
             else:
-                own_dq[at, lanes(g)] = dq
-
-        for band in range(BANDS):
-            body(band)
+                own_dq[band * OWN:(band + 1) * OWN, lanes(g)] = dqs[0].reshape(OWN, GW)
 
     column = lax.bitwise_and(iota((BANDS, QL), 1), 15)
-    spread_lon = onehot(TOKENS, 2 * EDGE, edge_index(iota((TOKENS, 2 * EDGE), 0), 0, RADIUS))
+    spread_lon = onehot(TOKENS, 2 * EDGE, edge_index(iota((TOKENS, 2 * EDGE), 0), 0, SIDE))
     mine = {}
     parts = {}
 
@@ -343,22 +384,21 @@
             qg[t, :, COLS:WIDE, lanes(g)] = got.reshape(ROWS, 16, GW)
         parts[g] = score(1, g)
         for d in range(2):
-            psend[g, d] = dot3(parts[g], pick_lanes(RADIUS if d == 0 else 0))
+            psend[g, d] = parts[g][:, (1 - d) * SL:(2 - d) * SL]
         for d in range(2):
             part_copy(g, d).start()
 
     def halo_grads(g):
-        theirs = jnp.zeros((3 * BANDS, QL), F32)
         for d in range(2):
             own_copy(g, d).wait_recv()
-            theirs = theirs + dot3(oland[g, d], put_lanes(d * RADIUS))
-        held = column < 2 * RADIUS
+        theirs = jnp.concatenate([oland[g, 0], oland[g, 1]], axis=1)
+        held = lax.bitwise_and(iota((BANDS, QL), 1), SIDE - 1) < RADIUS
         lse, delta = combine(parts[g], theirs, held)
         final[1, g, 0:BANDS, :] = jnp.where(held, lse, 0.0)
         final[1, g, BANDS:2 * BANDS, :] = jnp.where(held, delta, 0.0)
         grad(1, g)
         for d in range(2):
-            start = RADIUS if d == 0 else 0
+            start = SIDE if d == 0 else 0
             pick = onehot(EDGE, TOKENS, edge_token(iota((EDGE, TOKENS), 0), start))
             dsend[g, 0, d] = dot(pick, halo_dq[:, lanes(g)]).astype(BF16)
         for d in range(2):
@@ -374,8 +414,9 @@
         final[0, g, BANDS:2 * BANDS, :] = delta
         grad(0, g)
         for t in range(2):
-            lsend[g, 0, t] = acc[t, KEY_ROWS * COLS - RIM:, lanes(g)].astype(BF16)
-            lsend[g, 1, t] = acc[t, 0:RIM, lanes(g)].astype(BF16)
+            last = acc[t, RADIUS + ROWS:, :, lanes(g)]
+            lsend[g, 0, t] = last.reshape(RIM, GW).astype(BF16)
+            lsend[g, 1, t] = acc[t, 0:RADIUS, :, lanes(g)].reshape(RIM, GW).astype(BF16)
         start_lat(lat_back(g))
 
     own_scores(0)
@@ -397,16 +438,16 @@
     for g in range(PARTS):
         recv_lat(lat_back(g))
         for t, out in enumerate((dk_ref, dv_ref)):
-            first, last = RIM, RIM + TOKENS
-            top = acc[t, first:first + RIM, lanes(g)]
-            top = top + jnp.where(has_north, lland[g, 0, t].astype(F32), 0.0)
-            bottom = acc[t, last - RIM:last, lanes(g)]
-            bottom = bottom + jnp.where(has_south, lland[g, 1, t].astype(F32), 0.0)
-            middle = acc[t, first + RIM:last - RIM, lanes(g)]
-            out[0:RADIUS, :, lanes(g)] = top.astype(BF16).reshape(RADIUS, COLS, GW)
-            out[RADIUS:ROWS - RADIUS, :, lanes(g)] = middle.astype(BF16).reshape(
-                ROWS - 2 * RADIUS, COLS, GW)
-            out[ROWS - RADIUS:ROWS, :, lanes(g)] = bottom.astype(BF16).reshape(RADIUS, COLS, GW)
+            first, last = RADIUS, RADIUS + ROWS
+            rim = (RADIUS, COLS, GW)
+            top = lland[g, 0, t].astype(F32).reshape(rim)
+            top = acc[t, first:first + RADIUS, :, lanes(g)] + jnp.where(has_north, top, 0.0)
+            bottom = lland[g, 1, t].astype(F32).reshape(rim)
+            bottom = acc[t, last - RADIUS:last, :, lanes(g)] + jnp.where(has_south, bottom, 0.0)
+            middle = acc[t, first + RADIUS:last - RADIUS, :, lanes(g)]
+            out[0:RADIUS, :, lanes(g)] = top.astype(BF16)
+            out[RADIUS:ROWS - RADIUS, :, lanes(g)] = middle.astype(BF16)
+            out[ROWS - RADIUS:ROWS, :, lanes(g)] = bottom.astype(BF16)
 
     for g in range(PARTS):
         for d in range(2):
@@ -420,8 +461,11 @@
 
 
 def hand_on(*refs):
-    for i in range(3):
-        refs[3 + i][...] = refs[i][...]
+    copies = [pltpu.make_async_copy(refs[i], refs[3 + i], refs[6].at[i]) for i in range(3)]
+    for c in copies:
+        c.start()
+    for c in copies:
+        c.wait()
 
 
 def on_device(nlat, nlon, queries, keys, values, out_grad, pos_bias):
@@ -440,9 +484,12 @@
             pltpu.VMEM((2, KEY_ROWS, COLS, WIDTH), BF16),
             pltpu.VMEM((PARTS, 2, 2, EDGE, GW), BF16),
             pltpu.VMEM((PARTS, 2, 2, EDGE, GW), BF16),
-            pltpu.VMEM((2, NEAR, HEADS * OWN), F32),
-            pltpu.VMEM((2, PARTS * BANDS, NEAR, QL), F32),
-            pltpu.VMEM((2, PARTS * BANDS, NEAR, QL), F32),
+            pltpu.VMEM((NEAR, HEADS * OWN), F32),
+            pltpu.VMEM((2, DEEP * SIDE, HEADS * BAND * SIDE), F32),
+            pltpu.VMEM((PARTS * BANDS, NEAR, QL), F32),
+            pltpu.VMEM((PARTS * BANDS, 2, DEEP * SIDE, SL), F32),
+            pltpu.VMEM((PARTS * BANDS, 2, DEEP * SIDE, SL), F32),
+            pltpu.VMEM((PARTS * BANDS, NEAR, QL), F32),
             pltpu.VMEM((2, PARTS, 16, QL), F32),
             pltpu.VMEM((2, PARTS, 8, QL), F32),
             pltpu.VMEM((PARTS, 2, 3 * BANDS, 128), F32),
@@ -453,7 +500,7 @@
             pltpu.VMEM((TOKENS, WIDTH), BF16),
             pltpu.VMEM((PARTS, 1, 2, EDGE, GW), BF16),
             pltpu.VMEM((PARTS, 2, EDGE, GW), BF16),
-            pltpu.VMEM((2, KEY_ROWS * COLS, WIDTH), F32),
+            pltpu.VMEM((2, KEY_ROWS, COLS, WIDTH), F32),
             pltpu.VMEM((PARTS, 2, 2, RIM, GW), BF16),
             pltpu.VMEM((PARTS, 2, 2, RIM, GW), BF16),
             pltpu.VMEM((128, 128), F32),
@@ -470,7 +517,8 @@
         hand_on,
         out_shape=(block, block, block),
         in_specs=[vmem] * 3,
-        out_specs=(vmem,) * 3,
+        out_specs=(pl.BlockSpec(memory_space=pltpu.HBM),) * 3,
+        scratch_shapes=[dma((3,))],
         name="hand_on",
         compiler_params=pltpu.CompilerParams(vmem_limit_bytes=8 * 1024 * 1024),
     )(*grads)

time: 41.7 us -> 40.9 us (0.981)
  Pallas kernels: 41 us -> 40.1 us
    pallas_call x1, Pallas kernels: 40 us -> 39.2 us  [on_device(): pl.pallas_call(functools.partial(kernel, nlat, nlon), out_shape=(block, b...]
where the time goes in v1:
time: 40.9 us; the launch traced here: 40.7 us
  Pallas kernels  40.1 us (98%)
  between operations  0.64 us (2%)
    pallas_call x1, Pallas kernels, on_device(): pl.pallas_call(functools.partial(kernel, nlat, nlon), out_shape=(block, b...  39.2 us
    pallas_call x1, Pallas kernels, on_device(): pl.pallas_call(hand_on, out_shape=(block, block, block), in_specs=[vmem]...  0.9 us

profile of v1, /device:TPU:13, one launch (start us, length us, event | category | flops | bytes accessed | tf_op | source)
XLA Modules:
  0.0 40.7 jit_solution(4233593648091156278)
XLA Ops:
  0.6 39.2 %neighbourhood.1 = (bf16[16,16,512]{2,1,0:T(8,128)(2,1)S(1)}, bf16[16,16,512]{2,1,0:T(8,128)(2,1)S(1)}, bf16[16,16,512]{2,1,0:T(8,128)(2,1)S(1)}) custom-call(bf16[16,16,512]{2,1,0:T(8,128)(2,1)} %q_ref.1, bf16[16,16,512]{2,1,0:T(8,128)(2,1)} %k_ref.1, bf16[16,16,512]{2,1,0:T(8,128)(2,1)} %v_ref.1, bf16[16,16,512]{2,1,0:T(8,128)(2,1)} %g_ref.1, ...), custom_call_target="tpu_custom_call" | custom-call | tf_op jit(solution)/shard_map/neighbourhood/pallas_call | solution.py:477
  39.8 0.9 %hand_on.1 = (bf16[16,16,512]{2,1,0:T(8,128)(2,1)}, bf16[16,16,512]{2,1,0:T(8,128)(2,1)}, bf16[16,16,512]{2,1,0:T(8,128)(2,1)}) custom-call(bf16[16,16,512]{2,1,0:T(8,128)(2,1)S(1)} %get-tuple-element.6.refs_0_, bf16[16,16,512]{2,1,0:T(8,128)(2,1)S(1)} %get-tuple-element.7.refs_1_, bf16[16,16,512]{2,1,0:T(8,128)(2,1)S(1)} %get-tuple-element.8.refs_2_), custom_call_target="tpu_custom_call" | custom-call | tf_op jit(solution)/shard_map/hand_on/pallas_call | solution.py:516

commit v2 on v1

--- a/solution.py
+++ b/solution.py
@@ -155,15 +155,6 @@
             for g in range(PARTS):
                 dst[g, t, d] = got[:, lanes(g)]
 
-    for t in range(2):
-        loads[t].wait()
-        tokens = qg[t, :, 0:COLS, :].reshape(TOKENS, WIDTH)
-        pack_edges(send, t, tokens, (COLS - RADIUS, 0))
-    for c in loads[2:]:
-        c.wait()
-    peers = 2 + has_north.astype(jnp.int32) + has_south.astype(jnp.int32)
-    pl.semaphore_wait(bar, peers)
-
     along = (east, west)
     across = (south, north)
 
@@ -218,8 +209,16 @@
             for d in range(2):
                 lon_copy(g, t, d).start()
 
+    for c in loads[2:]:
+        c.wait()
+    peers = 2 + has_north.astype(jnp.int32) + has_south.astype(jnp.int32)
+    pl.semaphore_wait(bar, peers)
     start_lat(kv_mid(0))
     start_lat(kv_mid(1))
+    for t in range(2):
+        loads[t].wait()
+        tokens = qg[t, :, 0:COLS, :].reshape(TOKENS, WIDTH)
+        pack_edges(send, t, tokens, (COLS - RADIUS, 0))
     start_lon(0)
     start_lon(1)
 

time: 40.9 us -> 40.8 us (level)
  no operation moved by 1% of the time
where the time goes in v2:
time: 40.8 us; the launch traced here: 40.7 us
  Pallas kernels  40 us (98%)
  between operations  0.64 us (2%)
    pallas_call x1, Pallas kernels, on_device(): pl.pallas_call(functools.partial(kernel, nlat, nlon), out_shape=(block, b...  39.1 us
    pallas_call x1, Pallas kernels, on_device(): pl.pallas_call(hand_on, out_shape=(block, block, block), in_specs=[vmem]...  0.9 us

profile of v2, /device:TPU:13, one launch (start us, length us, event | category | flops | bytes accessed | tf_op | source)
XLA Modules:
  0.0 40.7 jit_solution(17475269836668288126)
XLA Ops:
  0.6 39.1 %neighbourhood.1 = (bf16[16,16,512]{2,1,0:T(8,128)(2,1)S(1)}, bf16[16,16,512]{2,1,0:T(8,128)(2,1)S(1)}, bf16[16,16,512]{2,1,0:T(8,128)(2,1)S(1)}) custom-call(bf16[16,16,512]{2,1,0:T(8,128)(2,1)} %q_ref.1, bf16[16,16,512]{2,1,0:T(8,128)(2,1)} %k_ref.1, bf16[16,16,512]{2,1,0:T(8,128)(2,1)} %v_ref.1, bf16[16,16,512]{2,1,0:T(8,128)(2,1)} %g_ref.1, ...), custom_call_target="tpu_custom_call" | custom-call | tf_op jit(solution)/shard_map/neighbourhood/pallas_call | solution.py:476
  39.8 0.9 %hand_on.1 = (bf16[16,16,512]{2,1,0:T(8,128)(2,1)}, bf16[16,16,512]{2,1,0:T(8,128)(2,1)}, bf16[16,16,512]{2,1,0:T(8,128)(2,1)}) custom-call(bf16[16,16,512]{2,1,0:T(8,128)(2,1)S(1)} %get-tuple-element.6.refs_0_, bf16[16,16,512]{2,1,0:T(8,128)(2,1)S(1)} %get-tuple-element.7.refs_1_, bf16[16,16,512]{2,1,0:T(8,128)(2,1)S(1)} %get-tuple-element.8.refs_2_), custom_call_target="tpu_custom_call" | custom-call | tf_op jit(solution)/shard_map/hand_on/pallas_call | solution.py:515
